TPU v7x, 128 devices: a whole 4x4x4 slice. The times are simulated.
128 devices in a mesh: row: 16 (over z, y), col: 8 (over x, core).
Axes of the slice: x: 4, y: 4, z: 4, core: 2. Of those that a mesh axis runs over, the one named last changes fastest.
Arguments:
- trailing: bfloat16 [24576, 24576], P('row', 'col'), may hold values from -6 to 6
- rows_a: int32 [16, 12], replicated, may hold values from 0 to 11, as said below
- counts_a: int32 [16], replicated, may hold values from 1 to 12, as said below
- factor_a: bfloat16 [24576, 512], P('row'), may hold values from -0.0390625 to 0.0390625
- rows_b: int32 [16, 12], replicated, may hold values from 0 to 11, as said below
- counts_b: int32 [16], replicated, may hold values from 1 to 12, as said below
- factor_b: bfloat16 [24576, 512], P('row'), may hold values from -0.0390625 to 0.0390625
- factor_top: bfloat16 [512, 512], replicated, may hold values from -0.25 to 0.25
- base_a: float32 [512, 512], P('col'), may hold values from -3 to 3
- base_b: float32 [512, 512], P('col'), may hold values from -3 to 3
Outputs:
- column_a: bfloat16 [24576, 512], P('row')
- diag_a: float32 [512, 512], P('col')
- column_b: bfloat16 [24576, 512], P('row')
- top_b: bfloat16 [512, 512], P('col')
- diag_b: float32 [512, 512], P('col')
Inputs may be any that keep to these rules, and one draw needn't show every extreme that they name: `rows_a`: the first counts_a[r] entries of row r are distinct; the rest of the row is padding. `counts_a`: some owner uses all 12 slots in every draw. `rows_b`: the first counts_b[r] entries of row r are distinct and lie among the first counts_a[r] entries of row r of rows_a; the rest is padding. counts_b[r] <= counts_a[r]; some owner uses all 12 slots in every draw.
All inputs are finite; a program needn't handle non-finite values.
Results may differ from a plain program's by a relative error of at most 0.007.
Values may be sent and summed in bfloat16 or wider, within the bound.
No kernel may reach another device: no remote copies, remote signals or barrier semaphores. Data moves between devices by JAX's collectives and lax.ppermute only.
A program may use at most 128 MiB of HBM per device.

v0:
```python
import jax
import jax.numpy as jnp
from jax import lax
from jax.sharding import PartitionSpec as P

BS = 128
W = 512
RBD = 12
PAD = 12


def spread_2(value, axis, source):
    kept = jnp.where(lax.axis_index(axis) == source, value, 0).astype(value.dtype)
    return lax.psum(kept, axis)


def contract_rows(former, latter):
    return lax.dot_general(
        former, latter, (((0,), (0,)), ((), ())), preferred_element_type=jnp.float32
    )


def slot_live(counts, owner_idx):
    live_count = lax.dynamic_index_in_dim(counts, owner_idx, 0, keepdims=False)
    return jnp.arange(PAD, dtype=jnp.int32) < live_count


def on_device(
    trailing, rows_a, counts_a, factor_a, rows_b, counts_b, factor_b, factor_top, base_a, base_b
):
    row_count = lax.axis_size("row")
    col_count = lax.axis_size("col")
    fanout = row_count // col_count
    row_index = lax.axis_index("row")
    col_index = lax.axis_index("col")
    col_blocks = trailing.shape[1] // BS
    part_width = W // col_count
    slot_rows = PAD * BS
    width_start = col_index * part_width
    slab_blocks = trailing.reshape(RBD, BS, trailing.shape[1])

    def row_gate(live_rows):
        return jnp.repeat(live_rows.astype(jnp.float32), BS)[:, None]

    def partial_product(rows, counts, factor):
        own_rows = lax.dynamic_index_in_dim(rows, row_index, 0, keepdims=False)
        row_slab = jnp.take(slab_blocks, own_rows, axis=0).reshape(slot_rows, trailing.shape[1])
        pieces = []
        targets = []
        flags = []
        for offset in range(fanout):
            source = col_index + offset * col_count
            pieces.append(spread_2(factor, "row", source))
            src_rows = lax.dynamic_index_in_dim(rows, source, 0, keepdims=False)
            targets.append(src_rows * fanout + offset)
            flags.append(slot_live(counts, source))
        received = jnp.stack(pieces).reshape(fanout * PAD, BS * W)
        target = jnp.concatenate(targets)
        live_src = jnp.concatenate(flags)
        selector = (
            (jnp.arange(col_blocks, dtype=jnp.int32)[:, None] == target[None, :])
            & live_src[None, :]
        ).astype(jnp.bfloat16)
        spread = jnp.dot(selector, received, preferred_element_type=jnp.float32).astype(
            jnp.bfloat16
        )
        return jnp.dot(
            row_slab, spread.reshape(col_blocks * BS, W), preferred_element_type=jnp.float32
        )

    def finish(partial_value, live_rows, addend):
        gate = row_gate(live_rows)
        summed = lax.psum(partial_value, "col")
        if addend is not None:
            summed = summed + addend(0, slot_rows)
        return (-summed * gate).astype(jnp.bfloat16)

    def row_sums(pieces_in):
        return lax.psum(pieces_in, "row")

    live_a = slot_live(counts_a, row_index)
    live_b = slot_live(counts_b, row_index)
    column_a = finish(partial_product(rows_a, counts_a, factor_a), live_a, None)
    own_rows_a = lax.dynamic_index_in_dim(rows_a, row_index, 0, keepdims=False)
    own_rows_b = lax.dynamic_index_in_dim(rows_b, row_index, 0, keepdims=False)
    pairing = (
        (own_rows_b[:, None] == own_rows_a[None, :]) & live_a[None, :] & live_b[:, None]
    ).astype(jnp.bfloat16)
    carried = (
        jnp.dot(pairing, column_a.reshape(PAD, BS * W), preferred_element_type=jnp.float32)
        .astype(jnp.bfloat16)
        .reshape(slot_rows, W)
    )
    width_a = lax.dynamic_slice_in_dim(column_a, width_start, part_width, 1)
    width_c = lax.dynamic_slice_in_dim(carried, width_start, part_width, 1)
    sums_a = row_sums((contract_rows(width_a, factor_a), contract_rows(width_c, factor_b)))
    diag_a = base_a - sums_a[0]
    top_b = (-(sums_a[1] + jnp.dot(diag_a, factor_top.astype(jnp.float32)))).astype(jnp.bfloat16)

    def cross_rows(first_row, row_total):
        return jnp.dot(carried, factor_top, preferred_element_type=jnp.float32)

    column_b = finish(partial_product(rows_b, counts_b, factor_b), live_b, cross_rows)
    width_b = lax.dynamic_slice_in_dim(column_b, width_start, part_width, 1)
    sums_b = row_sums((contract_rows(width_b, factor_b),))
    top_whole = lax.all_gather(top_b, "col", axis=0, tiled=True)
    top_cols = lax.dynamic_slice_in_dim(top_whole, width_start, part_width, 1)
    diag_b = base_b - sums_b[0] - contract_rows(top_cols, factor_top)
    return (column_a, diag_a, column_b, top_b, diag_b)


def solution(mesh):
    in_specs = (
        P("row", "col"),
        P(),
        P(),
        P("row", None),
        P(),
        P(),
        P("row", None),
        P(),
        P("col", None),
        P("col", None),
    )
    out_specs = (P("row", None), P("col", None), P("row", None), P("col", None), P("col", None))
    return jax.shard_map(
        on_device, mesh=mesh, in_specs=in_specs, out_specs=out_specs, check_vma=False
    )
```

profile of v0, /device:TPU:1, one launch (start us, length us, event | category | flops | bytes accessed | tf_op | source)
XLA Modules:
  0.0 408.7 jit_solution(16539790048383573170)
XLA Ops:
  7.2 4.8 %select_bitcast_fusion.1 = (bf16[1,1536,512]{2,1,0:T(8,128)(2,1)}, bf16[1,1536,512]{2,1,0:T(8,128)(2,1)}, bf16[1,1536,512]{2,1,0:T(8,128)(2,1)}, bf16[1,1536,512]{2,1,0:T(8,128)(2,1)}) fusion(bf16[1536,512]{1,0:T(8,128)(2,1)} %param.18, pred[]{:T(512)S(6)} %eq.50, pred[]{:T(512)S(6)} %eq.51, bf16[1536,512]{1,0:T(8,128)(2,1)} %param.15), kind=kLoop, calls=%fused_computation.15 | loop fusion | flops 3145728 | bytes 9437186 | tf_op jit(solution)/shard_map/stack | solution.py:57
  12.1 0.7 compare_and_fusion
  12.8 0.7 compare_and_fusion.1
  13.5 9.3 %gather_fusion.1 = bf16[12,128,3072]{2,1,0:T(8,128)(2,1)} fusion(bf16[12,128,3072]{2,1,0:T(8,128)(2,1)} %bitcast.50, s32[1024]{0:T(1024)S(1)} %pad_clamp_fusion), kind=kCustom, calls=%fused_computation.1.clone | custom fusion | bytes 18874416 | tf_op jit(solution)/shard_map/jit(_take)/gather | solution.py:47
  22.8 10.6 %gather_fusion = bf16[12,128,3072]{2,1,0:T(8,128)(2,1)} fusion(bf16[12,128,3072]{2,1,0:T(8,128)(2,1)} %bitcast.51, s32[1024]{0:T(1024)S(1)} %pad_clamp_fusion.1), kind=kCustom, calls=%fused_computation.clone | custom fusion | bytes 18874416 | tf_op jit(solution)/shard_map/jit(_take)/gather | solution.py:47
  33.4 0.7 fusion.47
  34.0 0.6 iota_compare_fusion.3
  34.7 0.7 iota_compare_fusion.4
  35.4 0.6 iota_compare_fusion.6
  36.0 0.6 iota_compare_fusion.7
  36.6 0.1 pad_add_fusion.1
  36.6 0.1 pad_add_fusion
  36.7 0.7 fusion.38
  37.4 0.7 fusion.33
  38.1 0.1 pad_add_fusion.2
  38.2 8.5 %broadcast_select_fusion = bf16[12,128,3072]{2,1,0:T(8,128)(2,1)} fusion(bf16[12,128,3072]{2,1,0:T(8,128)(2,1)} %gather_fusion.1, pred[12]{0:T(512)(128)(4,1)S(1)} %get-tuple-element.15), kind=kLoop, calls=%fused_computation.5 | loop fusion | flops 4718592 | bytes 18874380 | tf_op jit(solution)/shard_map/jit(_take)/select_n | solution.py:47
  46.7 8.6 %broadcast_select_fusion.1 = bf16[12,128,3072]{2,1,0:T(8,128)(2,1)} fusion(bf16[12,128,3072]{2,1,0:T(8,128)(2,1)} %gather_fusion, pred[12]{0:T(512)(128)(4,1)S(1)} %get-tuple-element.17), kind=kLoop, calls=%fused_computation.6 | loop fusion | flops 4718592 | bytes 18874380 | tf_op jit(solution)/shard_map/jit(_take)/select_n | solution.py:47
  55.3 83.3 %all-reduce.11.cloned.1.call-done = (bf16[1,1536,512]{2,1,0:T(8,128)(2,1)}, bf16[1,1536,512]{2,1,0:T(8,128)(2,1)}, bf16[1,1536,512]{2,1,0:T(8,128)(2,1)}, bf16[1,1536,512]{2,1,0:T(8,128)(2,1)}) async-done(((bf16[1,1536,512]{2,1,0:T(8,128)(2,1)}, bf16[1,1536,512]{2,1,0:T(8,128)(2,1)}, bf16[1,1536,512]{2,1,0:T(8,128)(2,1)}, bf16[1,1536,512]{2,1,0:T(8,128)(2,1)}), (bf16[1,1536,512]{2,1,0:T(8,128)(2,1)}, ...) | async-done | bytes 6291472 | tf_op jit(solution)/shard_map/psum | solution.py:14
  138.6 3.9 pad_maximum_fusion.1
  142.5 5.2 %reshape.75 = bf16[24,65536]{1,0:T(8,128)(2,1)} reshape(bf16[2,1536,512]{2,1,0:T(8,128)(2,1)} %pad_maximum_fusion.1) | data formatting | bytes 6291456 | tf_op jit(solution)/shard_map/reshape | solution.py:57
  147.7 4.5 %convolution_convert_fusion = bf16[24,65536]{1,0:T(8,128)(2,1)} fusion(bf16[24,65536]{1,0:T(8,128)(2,1)} %reshape.75, s32[24]{0:T(128)S(1)} %get-tuple-element.36, pred[24]{0:T(512)(128)(4,1)S(1)} %pad_add_fusion.1), kind=kOutput, calls=%fused_computation.2 | convolution fusion | flops 77071488 | bytes 6291576 | tf_op jit(solution)/shard_map/dot_general | solution.py:64
  152.2 5.3 %reshape.76 = bf16[3072,512]{1,0:T(8,128)(2,1)} reshape(bf16[24,65536]{1,0:T(8,128)(2,1)} %convolution_convert_fusion) | data formatting | bytes 6291456 | tf_op jit(solution)/shard_map/reshape | solution.py:68
  157.5 3.4 pad_maximum_fusion
  160.9 5.2 %reshape.72 = bf16[24,65536]{1,0:T(8,128)(2,1)} reshape(bf16[2,1536,512]{2,1,0:T(8,128)(2,1)} %pad_maximum_fusion) | data formatting | bytes 6291456 | tf_op jit(solution)/shard_map/reshape | solution.py:57
  166.1 4.5 %convolution_convert_fusion.1 = bf16[24,65536]{1,0:T(8,128)(2,1)} fusion(bf16[24,65536]{1,0:T(8,128)(2,1)} %reshape.72, s32[24]{0:T(128)S(1)} %get-tuple-element.35, pred[24]{0:T(512)(128)(4,1)S(1)} %pad_add_fusion), kind=kOutput, calls=%fused_computation.3 | convolution fusion | flops 77071488 | bytes 6291576 | tf_op jit(solution)/shard_map/dot_general | solution.py:64
  170.6 5.2 %reshape.73 = bf16[3072,512]{1,0:T(8,128)(2,1)} reshape(bf16[24,65536]{1,0:T(8,128)(2,1)} %convolution_convert_fusion.1) | data formatting | bytes 6291456 | tf_op jit(solution)/shard_map/reshape | solution.py:68
  175.9 10.8 %fusion.50 = f32[1536,512]{1,0:T(8,128)} fusion(bf16[1536,3072]{1,0:T(8,128)(2,1)} %bitcast.52, bf16[3072,512]{1,0:T(8,128)(2,1)} %reshape.76), kind=kOutput, calls=%fused_computation.89 | convolution fusion | flops 4831838208 | bytes 15728640 | tf_op jit(solution)/shard_map/dot_general | solution.py:67
  186.7 6.8 %fusion.49 = f32[1536,512]{1,0:T(8,128)} fusion(bf16[1536,3072]{1,0:T(8,128)(2,1)S(1)} %bitcast.55, bf16[3072,512]{1,0:T(8,128)(2,1)S(1)} %copy-done.3), kind=kOutput, calls=%fused_computation.88 | convolution fusion | flops 4831838208 | bytes 15728640 | tf_op jit(solution)/shard_map/dot_general | solution.py:67
  193.6 0.6 fusion.43
  194.2 0.6 iota_compare_fusion.5
  194.8 0.7 iota_compare_fusion.2
  195.5 0.7 fusion.44
  196.2 0.1 broadcast_bitcast_fusion.1
  196.3 81.0 %all-reduce.9.cloned.1.call-done = (f32[1536,512]{1,0:T(8,128)}, f32[1536,512]{1,0:T(8,128)}) async-done(((f32[1536,512]{1,0:T(8,128)}, f32[1536,512]{1,0:T(8,128)}), (f32[1536,512]{1,0:T(8,128)}, f32[1536,512]{1,0:T(8,128)})) %all-reduce.9.cloned.1.call-update) | async-done | bytes 6291472 | tf_op jit(solution)/shard_map/psum | solution.py:73
  277.3 3.5 multiply_convert_fusion
  280.8 2.2 reshape.77
  283.0 2.1 convolution_convert_fusion.2
  285.1 3.4 reshape.78
  288.5 2.9 fusion.9
  291.4 2.2 fusion.7
  293.6 2.9 fusion.2
  296.5 1.1 copy-done.4
  297.7 1.2 fusion.5
  298.9 83.9 %all-reduce.7.cloned.1.call-done = (f32[64,512]{1,0:T(8,128)}, f32[64,512]{1,0:T(8,128)}, f32[64,512]{1,0:T(8,128)}) async-done(((f32[64,512]{1,0:T(8,128)}, f32[64,512]{1,0:T(8,128)}, f32[64,512]{1,0:T(8,128)}), (f32[64,512]{1,0:T(8,128)}, f32[64,512]{1,0:T(8,128)}, f32[64,512]{1,0:T(8,128)})) %all-reduce.7.cloned.1.call-update) | async-done | bytes 393232 | tf_op jit(solution)/shard_map/psum | solution.py:79
  382.8 0.9 sub.9
  383.8 1.2 fusion.4
  385.0 15.4 %all_gather.3 = bf16[512,512]{1,0:T(8,128)(2,1)S(1)} all-gather(bf16[64,512]{1,0:T(8,128)(2,1)S(1)} %fusion.4), channel_id=1, replica_groups=mesh['row'=16,'col'=8] {'col'}, dimensions={0}, use_global_device_ids=true | all-gather | bytes 589824 | tf_op jit(solution)/shard_map/all_gather | solution.py:106
  400.3 1.9 convolution_subtract_fusion
  (40 shorter events, 0.3 us)
Async XLA Ops:
  7.2 286.4 %copy-start = (bf16[512,512]{1,0:T(8,128)(2,1)S(1)}, bf16[512,512]{1,0:T(8,128)(2,1)}, u32[]{:S(2)}) copy-start(bf16[512,512]{1,0:T(8,128)(2,1)} %param.19) | copy-start | bytes 1572868
  7.2 131.4 %all-reduce.11.cloned.1.call-start = ((), (), s32[]{:S(2)}) async-start(), calls=%async_computation.2 | async-start | bytes 12582912 | tf_op jit(solution)/shard_map/psum | solution.py:14
  12.0 265.3 %all-reduce.9.cloned.1.call-start = ((), (), s32[]{:S(2)}) async-start(), calls=%async_computation.1 | async-start | bytes 12582912 | tf_op jit(solution)/shard_map/psum | solution.py:73
  22.8 10.6 %copy-start.10 = (s32[16]{0:T(128)S(1)}, s32[16]{0:T(128)}, u32[]{:S(2)}) copy-start(s32[16]{0:T(128)} %param.17) | copy-start | bytes 196
  22.8 10.6 %copy-start.11 = (s32[16]{0:T(128)S(1)}, s32[16]{0:T(128)}, u32[]{:S(2)}) copy-start(s32[16]{0:T(128)} %param.14) | copy-start | bytes 196
  152.2 5.3 %copy-start.5 = (bf16[1,1536,512]{2,1,0:T(8,128)(2,1)S(1)}, bf16[1,1536,512]{2,1,0:T(8,128)(2,1)}, u32[]{:S(2)}) copy-start(bf16[1,1536,512]{2,1,0:T(8,128)(2,1)} %get-tuple-element.11) | copy-start | bytes 4718596
  170.6 16.0 %slice-start = ((s8[9437184]{0:T(1024)(128)(4,1)}), s8[1048576]{0:T(1024)(128)(4,1)S(1)}, s32[]{:S(2)}) async-start(s8[9437184]{0:T(1024)(128)(4,1)} %bitcast.53), calls=%async_computation.3 | async-start | bytes 2097152
  175.9 10.8 %slice-start.1 = ((s8[9437184]{0:T(1024)(128)(4,1)}), s8[4194304]{0:T(1024)(128)(4,1)S(1)}, s32[]{:S(2)}) async-start(s8[9437184]{0:T(1024)(128)(4,1)} %bitcast.53), calls=%async_computation.4 | async-start | bytes 8388608
  175.9 10.8 %slice-start.2 = ((s8[9437184]{0:T(1024)(128)(4,1)}), s8[4194304]{0:T(1024)(128)(4,1)S(1)}, s32[]{:S(2)}) async-start(s8[9437184]{0:T(1024)(128)(4,1)} %bitcast.53), calls=%async_computation.5 | async-start | bytes 8388608
  175.9 10.8 %copy-start.3 = (bf16[3072,512]{1,0:T(8,128)(2,1)S(1)}, bf16[3072,512]{1,0:T(8,128)(2,1)}, u32[]{:S(2)}) copy-start(bf16[3072,512]{1,0:T(8,128)(2,1)} %reshape.73) | copy-start | bytes 9437188
  193.5 189.3 %all-reduce.7.cloned.1.call-start = ((), (), s32[]{:S(2)}) async-start(), calls=%async_computation | async-start | bytes 786432 | tf_op jit(solution)/shard_map/psum | solution.py:79
  285.1 6.3 %copy-start.1 = (bf16[1536,512]{1,0:T(8,128)(2,1)S(1)}, bf16[1536,512]{1,0:T(8,128)(2,1)}, u32[]{:S(2)}) copy-start(bf16[1536,512]{1,0:T(8,128)(2,1)} %param.18) | copy-start | bytes 4718596
  288.5 5.1 %copy-start.2 = (bf16[1536,512]{1,0:T(8,128)(2,1)S(1)}, bf16[1536,512]{1,0:T(8,128)(2,1)}, u32[]{:S(2)}) copy-start(bf16[1536,512]{1,0:T(8,128)(2,1)} %reshape.78) | copy-start | bytes 4718596
  293.6 89.2 %copy-start.8 = (f32[64,512]{1,0:T(8,128)S(1)}, f32[64,512]{1,0:T(8,128)}, u32[]{:S(2)}) copy-start(f32[64,512]{1,0:T(8,128)} %param.20) | copy-start | bytes 393220
  296.5 1.1 copy-start.4
  297.7 102.7 %copy-start.9 = (f32[64,512]{1,0:T(8,128)S(1)}, f32[64,512]{1,0:T(8,128)}, u32[]{:S(2)}) copy-start(f32[64,512]{1,0:T(8,128)} %param.21) | copy-start | bytes 393220
  383.8 18.4 %copy-start.6 = (f32[64,512]{1,0:T(8,128)}, f32[64,512]{1,0:T(8,128)S(1)}, u32[]{:S(2)}) copy-start(f32[64,512]{1,0:T(8,128)S(1)} %sub.9) | copy-start | bytes 393220
  384.9 17.3 %copy-start.7 = (bf16[64,512]{1,0:T(8,128)(2,1)}, bf16[64,512]{1,0:T(8,128)(2,1)S(1)}, u32[]{:S(2)}) copy-start(bf16[64,512]{1,0:T(8,128)(2,1)S(1)} %fusion.4) | copy-start | bytes 196612
Sparse Core Ops, SparseCore 0:
  12.3 126.2 all-reduce.10
  193.6 83.6 all-reduce.8
  299.0 83.7 all-reduce.6
where the time goes:
time: 410 us; the launch traced here: 409 us
  waiting for transfers between devices  248 us (60%)
  local copies, waits for them, and re-layouts  48.5 us (12%)
  other arithmetic  41.6 us (10%)
  matrix products  41 us (10%)
  blocking collectives  15.4 us (4%)
  between operations  13.9 us (3%)
    psum x1, waiting for transfers between devices, row_sums(): return lax.psum(pieces_in, 'row')  83.9 us
    psum x1, waiting for transfers between devices, spread_2(): return lax.psum(kept, axis)  83.3 us
    psum x1, waiting for transfers between devices, finish(): summed = lax.psum(partial_value, 'col')  81 us
    gather x2, local copies, waits for them, and re-layouts, partial_product(): jnp.take(slab_blocks, own_rows, axis=0)  19.9 us
    dot_general x2, matrix products, partial_product(): jnp.dot(row_slab, spread.reshape(col_blocks * BS, W), preferred_element_t...  17.6 us
    select_n x3, other arithmetic, partial_product(): jnp.take(slab_blocks, own_rows, axis=0)  17.1 us
    all_gather x1, blocking collectives, on_device(): top_whole = lax.all_gather(top_b, 'col', axis=0, tiled=True)  15.4 us
    another operation x3, other arithmetic, partial_product(): received = jnp.stack(pieces).reshape(fanout * PAD, BS * W)  12 us
  transfers between devices with their start and end apart: 3, of which 3 were waited for; matrix products, arithmetic and copies ran while one was open for 11% of the time, Pallas kernels for 0%

commit v1 on v0

--- a/solution.py
+++ b/solution.py
@@ -70,7 +70,9 @@
 
     def finish(partial_value, live_rows, addend):
         gate = row_gate(live_rows)
-        summed = lax.psum(partial_value, "col")
+        summed = partial_value
+        for hop in (1, 2, 4):
+            summed = summed + lax.ppermute(summed, "col", [(dev, dev ^ hop) for dev in range(8)])
         if addend is not None:
             summed = summed + addend(0, slot_rows)
         return (-summed * gate).astype(jnp.bfloat16)

time: 410 us -> 585 us (1.43)
  waiting for transfers between devices: 248 us -> 402 us
  other arithmetic: 41.6 us -> 55.9 us
  starting transfers between devices: 0.12 us -> 8.77 us
    ppermute x0 -> x6, waiting for transfers between devices: none -> 239 us  [finish(): lax.ppermute(summed, 'col', [(dev, dev ^ hop) for dev in range(8)])]
    psum x1 -> x0, waiting for transfers between devices: 81 us -> none  [finish(): summed = lax.psum(partial_value, 'col')]
    ppermute x0 -> x6, starting transfers between devices: none -> 8.69 us  [finish(): lax.ppermute(summed, 'col', [(dev, dev ^ hop) for dev in range(8)])]
    add x0 -> x4, other arithmetic: none -> 8.49 us  [finish(): summed + lax.ppermute(summed, 'col', [(dev, dev ^ hop) for dev in range(8)])]
  transfers between devices with their start and end apart: 3 -> 8, of which waited for: 3 -> 7; matrix products, arithmetic and copies ran while one was open for 11% -> 16% of each run, Pallas kernels for 0% -> 0%
where the time goes in v1:
time: 585 us; the launch traced here: 584 us
  waiting for transfers between devices  402 us (69%)
  other arithmetic  55.9 us (10%)
  local copies, waits for them, and re-layouts  50.7 us (9%)
  matrix products  37 us (6%)
  blocking collectives  15.4 us (3%)
  between operations  14.3 us (2%)
  starting transfers between devices  8.77 us (1%)
    ppermute x6, waiting for transfers between devices, finish(): lax.ppermute(summed, 'col', [(dev, dev ^ hop) for dev in range(8)])  239 us
    psum x1, waiting for transfers between devices, spread_2(): return lax.psum(kept, axis)  83.1 us
    psum x1, waiting for transfers between devices, row_sums(): return lax.psum(pieces_in, 'row')  80.4 us
    gather x2, local copies, waits for them, and re-layouts, partial_product(): jnp.take(slab_blocks, own_rows, axis=0)  19.9 us
    dot_general x2, matrix products, partial_product(): jnp.dot(row_slab, spread.reshape(col_blocks * BS, W), preferred_element_t...  18.8 us
    select_n x3, other arithmetic, partial_product(): jnp.take(slab_blocks, own_rows, axis=0)  17.1 us
    all_gather x1, blocking collectives, on_device(): top_whole = lax.all_gather(top_b, 'col', axis=0, tiled=True)  15.4 us
    another operation x3, other arithmetic, partial_product(): received = jnp.stack(pieces).reshape(fanout * PAD, BS * W)  12 us
  transfers between devices with their start and end apart: 8, of which 7 were waited for; matrix products, arithmetic and copies ran while one was open for 16% of the time, Pallas kernels for 0%

profile of v1, /device:TPU:1, one launch (start us, length us, event | category | flops | bytes accessed | tf_op | source)
XLA Modules:
  0.0 584.1 jit_solution(8290184932295873139)
XLA Ops:
  7.2 4.8 select_bitcast_fusion.1
  12.1 0.7 compare_and_fusion.1
  13.5 9.3 %gather_fusion = bf16[12,128,3072]{2,1,0:T(8,128)(2,1)} fusion(bf16[12,128,3072]{2,1,0:T(8,128)(2,1)} %bitcast.50, s32[1024]{0:T(1024)S(1)} %pad_clamp_fusion.1), kind=kCustom, calls=%fused_computation.clone | custom fusion | bytes 18874416 | tf_op jit(solution)/shard_map/jit(_take)/gather | solution.py:47
  22.8 10.6 %gather_fusion.1 = bf16[12,128,3072]{2,1,0:T(8,128)(2,1)} fusion(bf16[12,128,3072]{2,1,0:T(8,128)(2,1)} %bitcast.51, s32[1024]{0:T(1024)S(1)} %pad_clamp_fusion), kind=kCustom, calls=%fused_computation.1.clone | custom fusion | bytes 18874416 | tf_op jit(solution)/shard_map/jit(_take)/gather | solution.py:47
  36.9 0.7 fusion.31
  37.6 0.7 fusion.36
  38.4 8.5 %broadcast_select_fusion.1 = bf16[12,128,3072]{2,1,0:T(8,128)(2,1)} fusion(bf16[12,128,3072]{2,1,0:T(8,128)(2,1)} %gather_fusion, pred[12]{0:T(512)(128)(4,1)S(1)} %get-tuple-element.25), kind=kLoop, calls=%fused_computation.6 | loop fusion | flops 4718592 | bytes 18874380 | tf_op jit(solution)/shard_map/jit(_take)/select_n | solution.py:47
  46.9 8.5 %broadcast_select_fusion = bf16[12,128,3072]{2,1,0:T(8,128)(2,1)} fusion(bf16[12,128,3072]{2,1,0:T(8,128)(2,1)} %gather_fusion.1, pred[12]{0:T(512)(128)(4,1)S(1)} %get-tuple-element.23), kind=kLoop, calls=%fused_computation.5 | loop fusion | flops 4718592 | bytes 18874380 | tf_op jit(solution)/shard_map/jit(_take)/select_n | solution.py:47
  55.4 83.1 %all-reduce.7.cloned.1.call-done = (bf16[1,1536,512]{2,1,0:T(8,128)(2,1)}, bf16[1,1536,512]{2,1,0:T(8,128)(2,1)}, bf16[1,1536,512]{2,1,0:T(8,128)(2,1)}, bf16[1,1536,512]{2,1,0:T(8,128)(2,1)}) async-done(((bf16[1,1536,512]{2,1,0:T(8,128)(2,1)}, bf16[1,1536,512]{2,1,0:T(8,128)(2,1)}, bf16[1,1536,512]{2,1,0:T(8,128)(2,1)}, bf16[1,1536,512]{2,1,0:T(8,128)(2,1)}), (bf16[1,1536,512]{2,1,0:T(8,128)(2,1)}, ...) | async-done | bytes 6291472 | tf_op jit(solution)/shard_map/psum | solution.py:14
  138.6 3.9 pad_maximum_fusion
  142.5 5.2 reshape.72
  147.7 4.6 convolution_convert_fusion.1
  152.3 5.4 reshape.73
  157.6 3.4 pad_maximum_fusion.1
  161.0 5.1 reshape.75
  166.2 10.1 %fusion.47 = f32[1536,512]{0,1:T(8,128)} fusion(bf16[1536,3072]{1,0:T(8,128)(2,1)} %bitcast.53, bf16[3072,512]{1,0:T(8,128)(2,1)} %reshape.73), kind=kOutput, calls=%fused_computation.86 | convolution fusion | flops 4831838208 | bytes 15728640 | tf_op jit(solution)/shard_map/dot_general | solution.py:67
  176.9 2.8 convolution_convert_fusion
  179.7 5.2 reshape.76
  184.9 8.7 %fusion.48 = f32[1536,512]{0,1:T(8,128)S(1)} fusion(bf16[1536,3072]{1,0:T(8,128)(2,1)} %bitcast.52, bf16[3072,512]{1,0:T(8,128)(2,1)} %reshape.76), kind=kOutput, calls=%fused_computation.87 | convolution fusion | flops 4831838208 | bytes 15728640 | tf_op jit(solution)/shard_map/dot_general | solution.py:67
  193.7 3.4 add.93
  197.1 1.3 collective-permute-start.1
  198.4 0.9 collective-permute-done.3
  199.9 1.3 collective-permute-start.4
  201.2 65.2 %collective-permute-done.1 = f32[1536,512]{0,1:T(8,128)S(1)} collective-permute-done((f32[1536,512]{0,1:T(8,128)S(1)}, f32[1536,512]{0,1:T(8,128)S(1)}, u32[]{:S(2)}, u32[]{:S(2)}) %collective-permute-start.1) | collective-permute-done | bytes 3145760 | tf_op jit(solution)/shard_map/ppermute | solution.py:75
  266.4 2.3 add.94
  268.6 2.7 collective-permute-start.2
  271.3 62.4 %collective-permute-done.4 = f32[1536,512]{0,1:T(8,128)S(1)} collective-permute-done((f32[1536,512]{0,1:T(8,128)S(1)}, f32[1536,512]{0,1:T(8,128)S(1)}, u32[]{:S(2)}, u32[]{:S(2)}) %collective-permute-start.4) | collective-permute-done | bytes 3145760 | tf_op jit(solution)/shard_map/ppermute | solution.py:75
  333.8 2.2 add.100
  336.0 2.7 collective-permute-start.5
  341.4 62.0 %collective-permute-done.2 = f32[1536,512]{0,1:T(8,128)} collective-permute-done((f32[1536,512]{0,1:T(8,128)}, f32[1536,512]{0,1:T(8,128)}, u32[]{:S(2)}, u32[]{:S(2)}) %collective-permute-start.2) | collective-permute-done | bytes 3145760 | tf_op jit(solution)/shard_map/ppermute | solution.py:75
  403.4 3.6 multiply_convert_fusion.1
  407.0 1.1 copy-done.3
  408.1 1.6 copy.18
  409.7 2.2 reshape.77
  411.9 2.2 convolution_convert_fusion.2
  414.1 2.5 reshape.78
  416.6 2.6 fusion.6
  419.2 2.6 fusion.2
  421.8 1.0 fusion.49
  422.9 48.0 %collective-permute-done.5 = f32[1536,512]{0,1:T(8,128)} collective-permute-done((f32[1536,512]{0,1:T(8,128)}, f32[1536,512]{0,1:T(8,128)}, u32[]{:S(2)}, u32[]{:S(2)}) %collective-permute-start.5) | collective-permute-done | bytes 3145760 | tf_op jit(solution)/shard_map/ppermute | solution.py:75
  470.8 4.0 multiply_convert_fusion
  474.8 1.0 fusion.4
  475.9 1.6 copy.19
  477.5 80.4 %all-reduce.5.cloned.1.call-done = (f32[64,512]{1,0:T(8,128)}, f32[64,512]{1,0:T(8,128)}, f32[64,512]{1,0:T(8,128)}) async-done(((f32[64,512]{1,0:T(8,128)}, f32[64,512]{1,0:T(8,128)}, f32[64,512]{1,0:T(8,128)}), (f32[64,512]{1,0:T(8,128)}, f32[64,512]{1,0:T(8,128)}, f32[64,512]{1,0:T(8,128)})) %all-reduce.5.cloned.1.call-update) | async-done | bytes 393232 | tf_op jit(solution)/shard_map/psum | solution.py:81
  557.8 0.9 sub.9
  558.8 1.2 fusion.1
  560.0 15.4 %all_gather.3 = bf16[512,512]{1,0:T(8,128)(2,1)S(1)} all-gather(bf16[64,512]{1,0:T(8,128)(2,1)S(1)} %fusion.1), channel_id=1, replica_groups=mesh['row'=16,'col'=8] {'col'}, dimensions={0}, use_global_device_ids=true | all-gather | bytes 589824 | tf_op jit(solution)/shard_map/all_gather | solution.py:108
  575.6 1.6 subtract_subtract_fusion
  (48 shorter events, 8.8 us)
Async XLA Ops:
  7.2 414.7 %copy-start = (bf16[512,512]{1,0:T(8,128)(2,1)S(1)}, bf16[512,512]{1,0:T(8,128)(2,1)}, u32[]{:S(2)}) copy-start(bf16[512,512]{1,0:T(8,128)(2,1)} %param.19) | copy-start | bytes 1572868
  7.2 131.4 %all-reduce.7.cloned.1.call-start = ((), (), s32[]{:S(2)}) async-start(), calls=%async_computation.1 | async-start | bytes 12582912 | tf_op jit(solution)/shard_map/psum | solution.py:14
  12.0 545.8 %all-reduce.5.cloned.1.call-start = ((), (), s32[]{:S(2)}) async-start(), calls=%async_computation | async-start | bytes 786432 | tf_op jit(solution)/shard_map/psum | solution.py:81
  22.7 10.6 %copy-start.9 = (s32[16]{0:T(128)S(1)}, s32[16]{0:T(128)}, u32[]{:S(2)}) copy-start(s32[16]{0:T(128)} %param.17) | copy-start | bytes 196
  22.8 10.6 %copy-start.10 = (s32[16]{0:T(128)S(1)}, s32[16]{0:T(128)}, u32[]{:S(2)}) copy-start(s32[16]{0:T(128)} %param.14) | copy-start | bytes 196
  152.3 5.4 copy-start.4
  166.2 10.7 %copy-start.2 = (bf16[24,65536]{1,0:T(8,128)(2,1)S(1)}, bf16[24,65536]{1,0:T(8,128)(2,1)}, u32[]{:S(2)}) copy-start(bf16[24,65536]{1,0:T(8,128)(2,1)} %reshape.75) | copy-start | bytes 9437188
  176.2 17.4 %collective-permute-start = (f32[1536,512]{0,1:T(8,128)}, f32[1536,512]{0,1:T(8,128)}, u32[]{:S(2)}, u32[]{:S(2)}) collective-permute-start(f32[1536,512]{0,1:T(8,128)} %fusion.47), channel_id=1, source_target_pairs={{0,1},{1,0},{2,3},{3,2},{4,5},{5,4},{6,7},{7,6},{8,9},{9,8},{10,11... | collective-permute-start | bytes 9437192 | tf_op jit(solution)/shard_map/ppermute | solution.py:75
  193.6 5.7 collective-permute-start.3
  197.1 69.3 %collective-permute-start.1 = (f32[1536,512]{0,1:T(8,128)S(1)}, f32[1536,512]{0,1:T(8,128)S(1)}, u32[]{:S(2)}, u32[]{:S(2)}) collective-permute-start(f32[1536,512]{0,1:T(8,128)S(1)} %add.93), channel_id=1, source_target_pairs={{0,2},{1,3},{2,0},{3,1},{4,6},{5,7},{6,4},{7,5},{8,10},{9,11},{10,... | collective-permute-start | bytes 9437192 | tf_op jit(solution)/shard_map/ppermute | solution.py:75
  199.9 133.9 %collective-permute-start.4 = (f32[1536,512]{0,1:T(8,128)S(1)}, f32[1536,512]{0,1:T(8,128)S(1)}, u32[]{:S(2)}, u32[]{:S(2)}) collective-permute-start(f32[1536,512]{0,1:T(8,128)S(1)} %add.99), channel_id=1, source_target_pairs={{0,2},{1,3},{2,0},{3,1},{4,6},{5,7},{6,4},{7,5},{8,10},{9,11},{10,... | collective-permute-start | bytes 9437192 | tf_op jit(solution)/shard_map/ppermute | solution.py:75
  268.6 134.8 %collective-permute-start.2 = (f32[1536,512]{0,1:T(8,128)}, f32[1536,512]{0,1:T(8,128)}, u32[]{:S(2)}, u32[]{:S(2)}) collective-permute-start(f32[1536,512]{0,1:T(8,128)} %add.94), channel_id=1, source_target_pairs={{0,4},{1,5},{2,6},{3,7},{4,0},{5,1},{6,2},{7,3},{8,12},{9,13},{10,... | collective-permute-start | bytes 9437192 | tf_op jit(solution)/shard_map/ppermute | solution.py:75
  336.0 134.9 %collective-permute-start.5 = (f32[1536,512]{0,1:T(8,128)}, f32[1536,512]{0,1:T(8,128)}, u32[]{:S(2)}, u32[]{:S(2)}) collective-permute-start(f32[1536,512]{0,1:T(8,128)} %add.100), channel_id=1, source_target_pairs={{0,4},{1,5},{2,6},{3,7},{4,0},{5,1},{6,2},{7,3},{8,12},{9,13},{10,... | collective-permute-start | bytes 9437192 | tf_op jit(solution)/shard_map/ppermute | solution.py:75
  407.0 1.1 copy-start.3
  422.9 51.9 %copy-start.1 = (bf16[1536,512]{1,0:T(8,128)(2,1)S(1)}, bf16[1536,512]{1,0:T(8,128)(2,1)}, u32[]{:S(2)}) copy-start(bf16[1536,512]{1,0:T(8,128)(2,1)} %param.18) | copy-start | bytes 4718596
  474.8 83.0 %copy-start.7 = (f32[64,512]{1,0:T(8,128)S(1)}, f32[64,512]{1,0:T(8,128)}, u32[]{:S(2)}) copy-start(f32[64,512]{1,0:T(8,128)} %param.20) | copy-start | bytes 393220
  475.9 99.8 %copy-start.8 = (f32[64,512]{1,0:T(8,128)S(1)}, f32[64,512]{1,0:T(8,128)}, u32[]{:S(2)}) copy-start(f32[64,512]{1,0:T(8,128)} %param.21) | copy-start | bytes 393220
  558.8 18.5 %copy-start.5 = (f32[64,512]{1,0:T(8,128)}, f32[64,512]{1,0:T(8,128)S(1)}, u32[]{:S(2)}) copy-start(f32[64,512]{1,0:T(8,128)S(1)} %sub.9) | copy-start | bytes 393220
  559.9 17.3 %copy-start.6 = (bf16[64,512]{1,0:T(8,128)(2,1)}, bf16[64,512]{1,0:T(8,128)(2,1)S(1)}, u32[]{:S(2)}) copy-start(bf16[64,512]{1,0:T(8,128)(2,1)S(1)} %fusion.1) | copy-start | bytes 196612
Sparse Core Ops, SparseCore 0:
  12.3 126.2 all-reduce.6
  476.0 81.7 all-reduce.4
